TPU v7x, 128 devices: a whole 4x4x4 slice. The times are simulated.
128 devices in a mesh: row: 8 (over z, x_lo), col: 16 (over x_hi, y, core).
Axes of the slice: x: 4 (x_hi: 2, x_lo: 2; x = x_hi * 2 + x_lo), y: 4, z: 4, core: 2. Of those that a mesh axis runs over, the one named last changes fastest.
Arguments:
- blocks: bfloat16 [8, 16, 192, 128, 128], P('row', 'col'), may hold values from -0.059814453 to 0.059814453
- block_rows: int32 [8, 16, 192], P('row', 'col'), may hold values from 0 to 255, as said below
- block_cols: int32 [8, 16, 192], P('row', 'col'), may hold values from 0 to 255, as said below
- counts: int32 [8, 16], P('row', 'col'), may hold values from 96 to 192, as said below
- travel_times: float32 [16, 262144], P(None, ('row', 'col')), may hold values from -6 to 6
Outputs:
- solution: float32 [16, 16, 8, 4096], P(None, 'col', 'row')
- scaled_direction: float32 [16, 16, 8, 4096], P(None, 'col', 'row')
Inputs may be any that keep to these rules, and one draw needn't show every extreme that they name: Ray block of a slot within the 256 ray blocks of its row group; among the filled slots of one device the (block_rows, block_cols) pairs are all different. `block_cols`: cell block of a slot within the 256 cell blocks of its column group. `counts`: some device fills all 192 slots.
All inputs are finite; a program needn't handle non-finite values.
Results may differ from a plain program's by a relative error of at most 0.0054.
Values may be sent and summed in bfloat16 or wider, within the bound.
No kernel may reach another device: no remote copies, remote signals or barrier semaphores. Data moves between devices by JAX's collectives and lax.ppermute only.
A program may use at most 64 MiB of HBM per device.

v0:
```python
import jax
import jax.numpy as jnp
from jax import lax
from jax.sharding import PartitionSpec as P

RB_DEV = 256
CB_DEV = 256
ITERS = 2
norm_eps = 1e-06


def rotation(rho_bar, phi_bar, beta_norm, alpha_norm):
    rho_new = jnp.sqrt(rho_bar * rho_bar + beta_norm * beta_norm)
    cosine = rho_bar / rho_new
    sine_val = beta_norm / rho_new
    theta_coef = sine_val * alpha_norm
    rho_next = -cosine * alpha_norm
    phi_new = cosine * phi_bar
    phi_next = sine_val * phi_bar
    return (phi_new / rho_new, theta_coef / rho_new, rho_next, phi_next)


def forward_rows(right_full, blocks_here, cols_here, row_hot):
    count_rhs = right_full.shape[0]
    block_size = blocks_here.shape[1]
    cells = right_full.reshape(count_rhs, right_full.shape[1] // block_size, block_size)
    picked = jnp.take(cells, cols_here, axis=1)
    product = jnp.einsum("knj,nij->kni", picked, blocks_here, preferred_element_type=jnp.float32)
    summed = jnp.einsum("rn,kni->kri", row_hot, product, precision=lax.Precision.HIGHEST)
    return summed.reshape(count_rhs, -1)


def backward_cols(left_full, blocks_here, rows_here, col_hot):
    count_rhs = left_full.shape[0]
    block_size = blocks_here.shape[1]
    rays = left_full.reshape(count_rhs, left_full.shape[1] // block_size, block_size)
    picked = jnp.take(rays, rows_here, axis=1)
    product = jnp.einsum("kni,nij->knj", picked, blocks_here, preferred_element_type=jnp.float32)
    summed = jnp.einsum("cn,knj->kcj", col_hot, product, precision=lax.Precision.HIGHEST)
    return summed.reshape(count_rhs, -1)


def square_sums(values):
    return jnp.sum(values * values, axis=1)


def shards(blocks, block_rows, block_cols, counts, travel_times):
    blocks_here = blocks[0, 0]
    rows_here = block_rows[0, 0]
    cols_here = block_cols[0, 0]
    slots = jnp.arange(blocks_here.shape[0], dtype=jnp.int32)
    filled = slots < counts[0, 0]
    row_hot = (
        (rows_here[None, :] == jnp.arange(RB_DEV, dtype=jnp.int32)[:, None]) & filled[None, :]
    ).astype(jnp.float32)
    col_hot = (
        (cols_here[None, :] == jnp.arange(CB_DEV, dtype=jnp.int32)[:, None]) & filled[None, :]
    ).astype(jnp.float32)
    count_rhs = travel_times.shape[0]

    def global_norm(partial_value):
        return jnp.sqrt(lax.psum(square_sums(partial_value), ("row", "col")) + norm_eps)

    def ray_side(partial_value):
        beta_norm = global_norm(partial_value)
        left_full = lax.all_gather(
            (partial_value / beta_norm[:, None]).astype(jnp.bfloat16), "col", axis=1, tiled=True
        )
        return (partial_value / beta_norm[:, None], left_full, beta_norm)

    def cell_side(partial_value):
        alpha_norm = global_norm(partial_value)
        right_full = None
        return (partial_value / alpha_norm[:, None], right_full, alpha_norm)

    def rows_to_cells(left_full):
        partial_value = backward_cols(left_full, blocks_here, rows_here, col_hot)
        return lax.psum_scatter(partial_value, "row", scatter_dimension=1, tiled=True)

    left_vec, left_full, beta_norm = ray_side(travel_times)
    right_vec, right_full, alpha_norm = cell_side(rows_to_cells(left_full))
    direction = right_vec
    solution = jnp.zeros_like(right_vec)
    phi_bar = beta_norm
    rho_bar = alpha_norm
    for iteration in range(ITERS):
        cells_right_full = lax.all_gather(right_vec.astype(jnp.bfloat16), "row", axis=1, tiled=True)
        cells_partial_value = forward_rows(cells_right_full, blocks_here, cols_here, row_hot)
        left_vec, left_full, beta_norm = ray_side(
            lax.psum_scatter(cells_partial_value, "col", scatter_dimension=1, tiled=True)
            - alpha_norm[:, None] * left_vec
        )
        right_vec, right_full, alpha_norm = cell_side(
            rows_to_cells(left_full) - beta_norm[:, None] * right_vec
        )
        step_scale, turn_scale, rho_bar, phi_bar = rotation(rho_bar, phi_bar, beta_norm, alpha_norm)
        solution = solution + step_scale[:, None] * direction
        direction = right_vec - turn_scale[:, None] * direction
    scaled = phi_bar[:, None] * direction
    return (solution.reshape(count_rhs, 1, 1, -1), scaled.reshape(count_rhs, 1, 1, -1))


def solution(mesh):
    placed = (
        P("row", "col", None, None, None),
        P("row", "col", None),
        P("row", "col", None),
        P("row", "col"),
        P(None, ("row", "col")),
    )
    return jax.shard_map(
        shards,
        mesh=mesh,
        in_specs=placed,
        out_specs=(P(None, "col", "row", None), P(None, "col", "row", None)),
        check_vma=False,
    )
```

profile of v0, /device:TPU:1, one launch (start us, length us, event | category | flops | bytes accessed | tf_op | source)
XLA Modules:
  0.0 989.8 jit_solution(17914631215639586107)
XLA Ops:
  8.2 68.7 %psum.42 = f32[16]{0:T(128)S(1)} all-reduce(f32[16]{0:T(128)S(1)} %multiply_reduce_fusion.5), channel_id=1, replica_groups=mesh['row'=8,'col'=16] {'row','col'}, use_global_device_ids=true, to_apply=%region_1.0 | all-reduce | flops 16 | bytes 128 | tf_op jit(solution)/shard_map/psum | solution.py:62
  80.7 39.5 %all-gather.6.cloned.1.call-done = bf16[16,32768]{1,0:T(8,128)(2,1)} async-done(((bf16[16,2048]{1,0:T(8,128)(2,1)}), bf16[16,32768]{1,0:T(8,128)(2,1)}) %all-gather.6.cloned.1.call-update) | async-done | bytes 1048592 | tf_op jit(solution)/shard_map/all_gather | solution.py:66
  122.3 3.9 fusion.15
  130.1 4.2 copy.65
  134.3 51.0 %reduce-scatter.6.cloned.1.call-done = f32[16,4096]{1,0:T(8,128)} async-done(((f32[16,32768]{1,0:T(8,128)}), f32[16,4096]{1,0:T(8,128)}) %reduce-scatter.6.cloned.1.call-update) | async-done | bytes 262160 | tf_op jit(solution)/shard_map/reduce_scatter | solution.py:78
  186.4 64.5 %psum.43 = f32[16]{0:T(128)S(1)} all-reduce(f32[16]{0:T(128)S(1)} %multiply_reduce_fusion.2), channel_id=1, replica_groups=mesh['row'=8,'col'=16] {'row','col'}, use_global_device_ids=true, to_apply=%region_4.6 | all-reduce | flops 16 | bytes 128 | tf_op jit(solution)/shard_map/psum | solution.py:62
  252.9 32.9 %all-gather.8.cloned.1.call-done = bf16[16,32768]{1,0:T(8,128)(2,1)} async-done(((bf16[16,4096]{1,0:T(8,128)(2,1)}), bf16[16,32768]{1,0:T(8,128)(2,1)}) %all-gather.8.cloned.1.call-update) | async-done | bytes 1048592 | tf_op jit(solution)/shard_map/all_gather | solution.py:87
  288.0 5.5 fusion.18
  297.3 4.2 copy.64
  301.6 73.0 %reduce-scatter.8.cloned.1.call-done = f32[16,2048]{1,0:T(8,128)} async-done(((f32[16,32768]{1,0:T(8,128)}), f32[16,2048]{1,0:T(8,128)}) %reduce-scatter.8.cloned.1.call-update) | async-done | bytes 131088 | tf_op jit(solution)/shard_map/reduce_scatter | solution.py:90
  375.7 66.4 %psum.44 = f32[16]{0:T(128)S(1)} all-reduce(f32[16]{0:T(128)S(1)} %get-tuple-element.17), channel_id=1, replica_groups=mesh['row'=8,'col'=16] {'row','col'}, use_global_device_ids=true, to_apply=%region_7.9 | all-reduce | flops 16 | bytes 128 | tf_op jit(solution)/shard_map/psum | solution.py:62
  442.9 41.6 %all-gather.10.cloned.1.call-done = bf16[16,32768]{1,0:T(8,128)(2,1)} async-done(((bf16[16,2048]{1,0:T(8,128)(2,1)}), bf16[16,32768]{1,0:T(8,128)(2,1)}) %all-gather.10.cloned.1.call-update) | async-done | bytes 1048592 | tf_op jit(solution)/shard_map/all_gather | solution.py:66
  494.4 4.2 copy.63
  498.6 51.0 %reduce-scatter.10.cloned.1.call-done = f32[16,4096]{1,0:T(8,128)} async-done(((f32[16,32768]{1,0:T(8,128)}), f32[16,4096]{1,0:T(8,128)}) %reduce-scatter.10.cloned.1.call-update) | async-done | bytes 262160 | tf_op jit(solution)/shard_map/reduce_scatter | solution.py:78
  550.8 64.8 %psum.45 = f32[16]{0:T(128)S(1)} all-reduce(f32[16]{0:T(128)S(1)} %multiply_reduce_fusion.1), channel_id=1, replica_groups=mesh['row'=8,'col'=16] {'row','col'}, use_global_device_ids=true, to_apply=%region_10.12 | all-reduce | flops 16 | bytes 128 | tf_op jit(solution)/shard_map/psum | solution.py:62
  617.4 33.1 %all-gather.12.cloned.1.call-done = bf16[16,32768]{1,0:T(8,128)(2,1)} async-done(((bf16[16,4096]{1,0:T(8,128)(2,1)}), bf16[16,32768]{1,0:T(8,128)(2,1)}) %all-gather.12.cloned.1.call-update) | async-done | bytes 1048592 | tf_op jit(solution)/shard_map/all_gather | solution.py:87
  652.7 5.5 fusion.24
  662.0 4.2 copy.62
  666.2 73.0 %reduce-scatter.12.cloned.1.call-done = f32[16,2048]{1,0:T(8,128)} async-done(((f32[16,32768]{1,0:T(8,128)}), f32[16,2048]{1,0:T(8,128)}) %reduce-scatter.12.cloned.1.call-update) | async-done | bytes 131088 | tf_op jit(solution)/shard_map/reduce_scatter | solution.py:90
  740.3 66.4 %psum.46 = f32[16]{0:T(128)S(1)} all-reduce(f32[16]{0:T(128)S(1)} %get-tuple-element.13), channel_id=1, replica_groups=mesh['row'=8,'col'=16] {'row','col'}, use_global_device_ids=true, to_apply=%region_13.15 | all-reduce | flops 16 | bytes 128 | tf_op jit(solution)/shard_map/psum | solution.py:62
  807.8 41.2 %all-gather.14.cloned.1.call-done = bf16[16,32768]{1,0:T(8,128)(2,1)} async-done(((bf16[16,2048]{1,0:T(8,128)(2,1)}), bf16[16,32768]{1,0:T(8,128)(2,1)}) %all-gather.14.cloned.1.call-update) | async-done | bytes 1048592 | tf_op jit(solution)/shard_map/all_gather | solution.py:66
  859.0 4.2 copy.61
  863.1 51.1 %reduce-scatter.14.cloned.1.call-done = f32[16,4096]{1,0:T(8,128)} async-done(((f32[16,32768]{1,0:T(8,128)}), f32[16,4096]{1,0:T(8,128)}) %reduce-scatter.14.cloned.1.call-update) | async-done | bytes 262160 | tf_op jit(solution)/shard_map/reduce_scatter | solution.py:78
  915.4 64.5 %psum.47 = f32[16]{0:T(128)S(1)} all-reduce(f32[16]{0:T(128)S(1)} %multiply_reduce_fusion), channel_id=1, replica_groups=mesh['row'=8,'col'=16] {'row','col'}, use_global_device_ids=true, to_apply=%region_16.18 | all-reduce | flops 16 | bytes 128 | tf_op jit(solution)/shard_map/psum | solution.py:62
  (77 shorter events, 56.6 us)
Async XLA Ops:
  7.2 113.0 %all-gather.6.cloned.1.call-start = ((), (), s32[]{:S(2)}) async-start(), calls=%async_computation.5 | async-start | bytes 1114112 | tf_op jit(solution)/shard_map/all_gather | solution.py:66
  78.6 106.7 %reduce-scatter.6.cloned.1.call-start = ((), (), s32[]{:S(2)}) async-start(), calls=%async_computation.6 | async-start | bytes 2359296 | tf_op jit(solution)/shard_map/reduce_scatter | solution.py:78
  122.3 3.9 copy-start.2
  134.3 151.6 %all-gather.8.cloned.1.call-start = ((), (), s32[]{:S(2)}) async-start(), calls=%async_computation.7 | async-start | bytes 1179648 | tf_op jit(solution)/shard_map/all_gather | solution.py:87
  252.7 121.9 %reduce-scatter.8.cloned.1.call-start = ((), (), s32[]{:S(2)}) async-start(), calls=%async_computation.8 | async-start | bytes 2228224 | tf_op jit(solution)/shard_map/reduce_scatter | solution.py:90
  288.0 5.5 copy-start.3
  301.5 73.1 %copy-start.1 = (f32[16,2048]{1,0:T(8,128)S(1)}, f32[16,2048]{1,0:T(8,128)}, u32[]{:S(2)}) copy-start(f32[16,2048]{1,0:T(8,128)} %param.11) | copy-start | bytes 393220
  301.5 183.0 %all-gather.10.cloned.1.call-start = ((), (), s32[]{:S(2)}) async-start(), calls=%async_computation.9 | async-start | bytes 1114112 | tf_op jit(solution)/shard_map/all_gather | solution.py:66
  442.9 106.8 %reduce-scatter.10.cloned.1.call-start = ((), (), s32[]{:S(2)}) async-start(), calls=%async_computation.10 | async-start | bytes 2359296 | tf_op jit(solution)/shard_map/reduce_scatter | solution.py:78
  498.6 51.1 %copy-start = (f32[16,4096]{1,0:T(8,128)S(1)}, f32[16,4096]{1,0:T(8,128)}, u32[]{:S(2)}) copy-start(f32[16,4096]{1,0:T(8,128)} %reduce-scatter.6.cloned.1.call-done) | copy-start | bytes 786436
  498.6 151.9 %all-gather.12.cloned.1.call-start = ((), (), s32[]{:S(2)}) async-start(), calls=%async_computation.11 | async-start | bytes 1179648 | tf_op jit(solution)/shard_map/all_gather | solution.py:87
  617.3 121.9 %reduce-scatter.12.cloned.1.call-start = ((), (), s32[]{:S(2)}) async-start(), calls=%async_computation.12 | async-start | bytes 2228224 | tf_op jit(solution)/shard_map/reduce_scatter | solution.py:90
  666.2 182.9 %all-gather.14.cloned.1.call-start = ((), (), s32[]{:S(2)}) async-start(), calls=%async_computation.13 | async-start | bytes 1114112 | tf_op jit(solution)/shard_map/all_gather | solution.py:66
  807.5 106.7 %reduce-scatter.14.cloned.1.call-start = ((), (), s32[]{:S(2)}) async-start(), calls=%async_computation.14 | async-start | bytes 2359296 | tf_op jit(solution)/shard_map/reduce_scatter | solution.py:78
Sparse Core Ops, SparseCore 0:
  78.7 41.3 all-gather.5
  134.4 50.8 reduce-scatter.5
  252.8 32.9 all-gather.7
  301.7 72.8 reduce-scatter.7
  443.0 41.4 all-gather.9
  498.7 50.8 reduce-scatter.9
  617.4 32.9 all-gather.11
  666.3 72.8 reduce-scatter.11
  807.6 41.3 all-gather.13
  863.3 50.8 reduce-scatter.13
where the time goes:
time: 991 us; the launch traced here: 990 us
  waiting for transfers between devices  487 us (49%)
  blocking collectives  395 us (40%)
  local copies, waits for them, and re-layouts  42.8 us (4%)
  matrix products  32.6 us (3%)
  other arithmetic  15.8 us (2%)
  between operations  15 us (2%)
    psum x6, blocking collectives, global_norm(): lax.psum(square_sums(partial_value), ('row', 'col')) + norm_eps  395 us
    reduce_scatter x3, waiting for transfers between devices, rows_to_cells(): lax.psum_scatter(partial_value, 'row', scatter_dimension=1, tiled=True)  153 us
    reduce_scatter x2, waiting for transfers between devices, shards(): lax.psum_scatter(cells_partial_value, 'col', scatter_dimension=1, tiled=T...  146 us
    all_gather x3, waiting for transfers between devices, ray_side(): lax.all_gather((partial_value / beta_norm[:, None]).astype(jnp.bfloat16),...  122 us
    all_gather x2, waiting for transfers between devices, shards(): lax.all_gather(right_vec.astype(jnp.bfloat16), 'row', axis=1, tiled=True)  66 us
    unnamed x15, local copies, waits for them, and re-layouts  22.8 us
  transfers between devices with their start and end apart: 10, of which 10 were waited for; matrix products, arithmetic and copies ran while one was open for 0% of the time, Pallas kernels for 0%

commit v1 on v0

--- a/solution.py
+++ b/solution.py
@@ -59,7 +59,7 @@
     count_rhs = travel_times.shape[0]
 
     def global_norm(partial_value):
-        return jnp.sqrt(lax.psum(square_sums(partial_value), ("row", "col")) + norm_eps)
+        return jnp.sqrt(lax.psum(lax.psum(square_sums(partial_value), "col"), "row") + norm_eps)
 
     def ray_side(partial_value):
         beta_norm = global_norm(partial_value)

time: 991 us -> 918 us (0.926)
  blocking collectives: 395 us -> 293 us
  waiting for transfers between devices: 487 us -> 511 us
    psum x6 -> x12, blocking collectives: 395 us -> 293 us  [the longest x6 205 us: global_norm(): lax.psum(square_sums(partial_value), 'col')]
    all_gather x3, waiting for transfers between devices: 122 us -> 136 us  [ray_side(): lax.all_gather((partial_value / beta_norm[:, None]).astype(jnp.bfloat16),...]
    all_gather x2, waiting for transfers between devices: 66 us -> 76.1 us  [shards(): lax.all_gather(right_vec.astype(jnp.bfloat16), 'row', axis=1, tiled=True)]
where the time goes in v1:
time: 918 us; the launch traced here: 911 us
  waiting for transfers between devices  511 us (56%)
  blocking collectives  293 us (32%)
  local copies, waits for them, and re-layouts  42.8 us (5%)
  matrix products  32.6 us (4%)
  other arithmetic  15.8 us (2%)
  between operations  15 us (2%)
    psum x6, blocking collectives, global_norm(): lax.psum(square_sums(partial_value), 'col')  205 us
    reduce_scatter x3, waiting for transfers between devices, rows_to_cells(): lax.psum_scatter(partial_value, 'row', scatter_dimension=1, tiled=True)  153 us
    reduce_scatter x2, waiting for transfers between devices, shards(): lax.psum_scatter(cells_partial_value, 'col', scatter_dimension=1, tiled=T...  146 us
    all_gather x3, waiting for transfers between devices, ray_side(): lax.all_gather((partial_value / beta_norm[:, None]).astype(jnp.bfloat16),...  136 us
    psum x6, blocking collectives, global_norm(): lax.psum(lax.psum(square_sums(partial_value), 'col'), 'row') + norm_eps  87.8 us
    all_gather x2, waiting for transfers between devices, shards(): lax.all_gather(right_vec.astype(jnp.bfloat16), 'row', axis=1, tiled=True)  76.1 us
    unnamed x15, local copies, waits for them, and re-layouts  22.8 us
  transfers between devices with their start and end apart: 10, of which 10 were waited for; matrix products, arithmetic and copies ran while one was open for 0% of the time, Pallas kernels for 0%

profile of v1, /device:TPU:1, one launch (start us, length us, event | category | flops | bytes accessed | tf_op | source)
XLA Modules:
  0.0 910.9 jit_solution(13013864317404463534)
XLA Ops:
  8.2 34.2 %psum.84 = f32[16]{0:T(128)S(1)} all-reduce(f32[16]{0:T(128)S(1)} %multiply_reduce_fusion.5), channel_id=1, replica_groups=mesh['row'=8,'col'=16] {'col'}, use_global_device_ids=true, to_apply=%region_1.0 | all-reduce | flops 16 | bytes 128 | tf_op jit(solution)/shard_map/psum | solution.py:62
  42.5 17.0 %psum.85 = f32[16]{0:T(128)S(1)} all-reduce(f32[16]{0:T(128)S(1)} %psum.84), channel_id=1, replica_groups=mesh['row'=8,'col'=16] {'row'}, use_global_device_ids=true, to_apply=%region_2.0 | all-reduce | flops 16 | bytes 128 | tf_op jit(solution)/shard_map/psum | solution.py:62
  63.2 46.1 %all-gather.6.cloned.1.call-done = bf16[16,32768]{1,0:T(8,128)(2,1)} async-done(((bf16[16,2048]{1,0:T(8,128)(2,1)}), bf16[16,32768]{1,0:T(8,128)(2,1)}) %all-gather.6.cloned.1.call-update) | async-done | bytes 1048592 | tf_op jit(solution)/shard_map/all_gather | solution.py:66
  123.4 51.0 %reduce-scatter.6.cloned.1.call-done = f32[16,4096]{1,0:T(8,128)} async-done(((f32[16,32768]{1,0:T(8,128)}), f32[16,4096]{1,0:T(8,128)}) %reduce-scatter.6.cloned.1.call-update) | async-done | bytes 262160 | tf_op jit(solution)/shard_map/reduce_scatter | solution.py:78
  175.5 33.6 %psum.86 = f32[16]{0:T(128)S(1)} all-reduce(f32[16]{0:T(128)S(1)} %multiply_reduce_fusion.2), channel_id=1, replica_groups=mesh['row'=8,'col'=16] {'col'}, use_global_device_ids=true, to_apply=%region_5.7 | all-reduce | flops 16 | bytes 128 | tf_op jit(solution)/shard_map/psum | solution.py:62
  209.1 13.3 %psum.87 = f32[16]{0:T(128)S(1)} all-reduce(f32[16]{0:T(128)S(1)} %psum.86), channel_id=1, replica_groups=mesh['row'=8,'col'=16] {'row'}, use_global_device_ids=true, to_apply=%region_6.8 | all-reduce | flops 16 | bytes 128 | tf_op jit(solution)/shard_map/psum | solution.py:62
  224.3 38.0 %all-gather.8.cloned.1.call-done = bf16[16,32768]{1,0:T(8,128)(2,1)} async-done(((bf16[16,4096]{1,0:T(8,128)(2,1)}), bf16[16,32768]{1,0:T(8,128)(2,1)}) %all-gather.8.cloned.1.call-update) | async-done | bytes 1048592 | tf_op jit(solution)/shard_map/all_gather | solution.py:87
  264.5 5.5 fusion.18
  278.1 73.0 %reduce-scatter.8.cloned.1.call-done = f32[16,2048]{1,0:T(8,128)} async-done(((f32[16,32768]{1,0:T(8,128)}), f32[16,2048]{1,0:T(8,128)}) %reduce-scatter.8.cloned.1.call-update) | async-done | bytes 131088 | tf_op jit(solution)/shard_map/reduce_scatter | solution.py:90
  352.2 35.1 %psum.88 = f32[16]{0:T(128)S(1)} all-reduce(f32[16]{0:T(128)S(1)} %get-tuple-element.17), channel_id=1, replica_groups=mesh['row'=8,'col'=16] {'col'}, use_global_device_ids=true, to_apply=%region_9.11 | all-reduce | flops 16 | bytes 128 | tf_op jit(solution)/shard_map/psum | solution.py:62
  387.3 15.4 %psum.89 = f32[16]{0:T(128)S(1)} all-reduce(f32[16]{0:T(128)S(1)} %psum.88), channel_id=1, replica_groups=mesh['row'=8,'col'=16] {'row'}, use_global_device_ids=true, to_apply=%region_10.12 | all-reduce | flops 16 | bytes 128 | tf_op jit(solution)/shard_map/psum | solution.py:62
  403.7 44.8 %all-gather.10.cloned.1.call-done = bf16[16,32768]{1,0:T(8,128)(2,1)} async-done(((bf16[16,2048]{1,0:T(8,128)(2,1)}), bf16[16,32768]{1,0:T(8,128)(2,1)}) %all-gather.10.cloned.1.call-update) | async-done | bytes 1048592 | tf_op jit(solution)/shard_map/all_gather | solution.py:66
  462.6 51.0 %reduce-scatter.10.cloned.1.call-done = f32[16,4096]{1,0:T(8,128)} async-done(((f32[16,32768]{1,0:T(8,128)}), f32[16,4096]{1,0:T(8,128)}) %reduce-scatter.10.cloned.1.call-update) | async-done | bytes 262160 | tf_op jit(solution)/shard_map/reduce_scatter | solution.py:78
  514.8 33.6 %psum.90 = f32[16]{0:T(128)S(1)} all-reduce(f32[16]{0:T(128)S(1)} %multiply_reduce_fusion.1), channel_id=1, replica_groups=mesh['row'=8,'col'=16] {'col'}, use_global_device_ids=true, to_apply=%region_13.15 | all-reduce | flops 16 | bytes 128 | tf_op jit(solution)/shard_map/psum | solution.py:62
  548.4 13.3 %psum.91 = f32[16]{0:T(128)S(1)} all-reduce(f32[16]{0:T(128)S(1)} %psum.90), channel_id=1, replica_groups=mesh['row'=8,'col'=16] {'row'}, use_global_device_ids=true, to_apply=%region_14.16 | all-reduce | flops 16 | bytes 128 | tf_op jit(solution)/shard_map/psum | solution.py:62
  563.5 38.1 %all-gather.12.cloned.1.call-done = bf16[16,32768]{1,0:T(8,128)(2,1)} async-done(((bf16[16,4096]{1,0:T(8,128)(2,1)}), bf16[16,32768]{1,0:T(8,128)(2,1)}) %all-gather.12.cloned.1.call-update) | async-done | bytes 1048592 | tf_op jit(solution)/shard_map/all_gather | solution.py:87
  603.8 5.5 fusion.24
  617.4 73.0 %reduce-scatter.12.cloned.1.call-done = f32[16,2048]{1,0:T(8,128)} async-done(((f32[16,32768]{1,0:T(8,128)}), f32[16,2048]{1,0:T(8,128)}) %reduce-scatter.12.cloned.1.call-update) | async-done | bytes 131088 | tf_op jit(solution)/shard_map/reduce_scatter | solution.py:90
  691.5 35.1 %psum.92 = f32[16]{0:T(128)S(1)} all-reduce(f32[16]{0:T(128)S(1)} %get-tuple-element.13), channel_id=1, replica_groups=mesh['row'=8,'col'=16] {'col'}, use_global_device_ids=true, to_apply=%region_17.19 | all-reduce | flops 16 | bytes 128 | tf_op jit(solution)/shard_map/psum | solution.py:62
  726.6 15.4 %psum.93 = f32[16]{0:T(128)S(1)} all-reduce(f32[16]{0:T(128)S(1)} %psum.92), channel_id=1, replica_groups=mesh['row'=8,'col'=16] {'row'}, use_global_device_ids=true, to_apply=%region_18.20 | all-reduce | flops 16 | bytes 128 | tf_op jit(solution)/shard_map/psum | solution.py:62
  743.0 44.7 %all-gather.14.cloned.1.call-done = bf16[16,32768]{1,0:T(8,128)(2,1)} async-done(((bf16[16,2048]{1,0:T(8,128)(2,1)}), bf16[16,32768]{1,0:T(8,128)(2,1)}) %all-gather.14.cloned.1.call-update) | async-done | bytes 1048592 | tf_op jit(solution)/shard_map/all_gather | solution.py:66
  801.8 51.1 %reduce-scatter.14.cloned.1.call-done = f32[16,4096]{1,0:T(8,128)} async-done(((f32[16,32768]{1,0:T(8,128)}), f32[16,4096]{1,0:T(8,128)}) %reduce-scatter.14.cloned.1.call-update) | async-done | bytes 262160 | tf_op jit(solution)/shard_map/reduce_scatter | solution.py:78
  854.1 33.6 %psum.94 = f32[16]{0:T(128)S(1)} all-reduce(f32[16]{0:T(128)S(1)} %multiply_reduce_fusion), channel_id=1, replica_groups=mesh['row'=8,'col'=16] {'col'}, use_global_device_ids=true, to_apply=%region_21.23 | all-reduce | flops 16 | bytes 128 | tf_op jit(solution)/shard_map/psum | solution.py:62
  887.6 13.3 %psum.95 = f32[16]{0:T(128)S(1)} all-reduce(f32[16]{0:T(128)S(1)} %psum.94), channel_id=1, replica_groups=mesh['row'=8,'col'=16] {'row'}, use_global_device_ids=true, to_apply=%region_22.24 | all-reduce | flops 16 | bytes 128 | tf_op jit(solution)/shard_map/psum | solution.py:62
  (83 shorter events, 81.2 us)
Async XLA Ops:
  7.2 102.1 %all-gather.6.cloned.1.call-start = ((), (), s32[]{:S(2)}) async-start(), calls=%async_computation.5 | async-start | bytes 1114112 | tf_op jit(solution)/shard_map/all_gather | solution.py:66
  61.1 113.3 %reduce-scatter.6.cloned.1.call-start = ((), (), s32[]{:S(2)}) async-start(), calls=%async_computation.6 | async-start | bytes 2359296 | tf_op jit(solution)/shard_map/reduce_scatter | solution.py:78
  111.5 3.9 copy-start.2
  123.4 138.9 %all-gather.8.cloned.1.call-start = ((), (), s32[]{:S(2)}) async-start(), calls=%async_computation.7 | async-start | bytes 1179648 | tf_op jit(solution)/shard_map/all_gather | solution.py:87
  224.2 126.9 %reduce-scatter.8.cloned.1.call-start = ((), (), s32[]{:S(2)}) async-start(), calls=%async_computation.8 | async-start | bytes 2228224 | tf_op jit(solution)/shard_map/reduce_scatter | solution.py:90
  264.5 5.5 copy-start.3
  278.0 73.1 %copy-start.1 = (f32[16,2048]{1,0:T(8,128)S(1)}, f32[16,2048]{1,0:T(8,128)}, u32[]{:S(2)}) copy-start(f32[16,2048]{1,0:T(8,128)} %param.11) | copy-start | bytes 393220
  278.0 170.4 %all-gather.10.cloned.1.call-start = ((), (), s32[]{:S(2)}) async-start(), calls=%async_computation.9 | async-start | bytes 1114112 | tf_op jit(solution)/shard_map/all_gather | solution.py:66
  403.5 110.2 %reduce-scatter.10.cloned.1.call-start = ((), (), s32[]{:S(2)}) async-start(), calls=%async_computation.10 | async-start | bytes 2359296 | tf_op jit(solution)/shard_map/reduce_scatter | solution.py:78
  462.5 51.1 %copy-start = (f32[16,4096]{1,0:T(8,128)S(1)}, f32[16,4096]{1,0:T(8,128)}, u32[]{:S(2)}) copy-start(f32[16,4096]{1,0:T(8,128)} %reduce-scatter.6.cloned.1.call-done) | copy-start | bytes 786436
  462.6 139.0 %all-gather.12.cloned.1.call-start = ((), (), s32[]{:S(2)}) async-start(), calls=%async_computation.11 | async-start | bytes 1179648 | tf_op jit(solution)/shard_map/all_gather | solution.py:87
  563.5 126.9 %reduce-scatter.12.cloned.1.call-start = ((), (), s32[]{:S(2)}) async-start(), calls=%async_computation.12 | async-start | bytes 2228224 | tf_op jit(solution)/shard_map/reduce_scatter | solution.py:90
  617.3 170.4 %all-gather.14.cloned.1.call-start = ((), (), s32[]{:S(2)}) async-start(), calls=%async_computation.13 | async-start | bytes 1114112 | tf_op jit(solution)/shard_map/all_gather | solution.py:66
  742.8 110.1 %reduce-scatter.14.cloned.1.call-start = ((), (), s32[]{:S(2)}) async-start(), calls=%async_computation.14 | async-start | bytes 2359296 | tf_op jit(solution)/shard_map/reduce_scatter | solution.py:78
Sparse Core Ops, SparseCore 0:
  61.2 47.9 all-gather.5
  123.5 50.8 reduce-scatter.5
  224.3 37.9 all-gather.7
  278.1 72.8 reduce-scatter.7
  403.6 44.8 all-gather.9
  462.7 50.8 reduce-scatter.9
  563.6 37.9 all-gather.11
  617.4 72.8 reduce-scatter.11
  742.9 44.8 all-gather.13
  802.0 50.8 reduce-scatter.13
